TPU v7x, 128 devices: a whole 4x4x4 slice. The times are simulated.
128 devices in a mesh: rep: 16 (over z_hi, x, core), sp: 8 (over z_lo, y).
Axes of the slice: x: 4, y: 4, z: 4 (z_hi: 2, z_lo: 2; z = z_hi * 2 + z_lo), core: 2. Of those that a mesh axis runs over, the one named last changes fastest.
Arguments:
- positions: float32 [16, 3, 65536], P('rep', None, 'sp'), may hold values from -18 to 18
- velocities: float32 [16, 3, 65536], P('rep', None, 'sp'), may hold values from -6 to 6
- strength: float32 [16, 65536], P('rep', 'sp'), may hold values from 0.5 to 2
- inv_mass: float32 [16, 65536], P('rep', 'sp'), may hold values from 0.1 to 1
- tile_lists: int32 [16, 4, 512, 4], P('rep', None, 'sp'), may hold values from 0 to 127, as said below
- solute_index: int32 [16, 2048], P('rep', 'sp'), may hold values from 0 to 8191, as said below
- scatter_weight: float32 [16, 2048], P('rep', 'sp'), may hold values from 0.3 to 3
- intensity_exp: float32 [48], replicated, may hold values from 0.5 to 3
- precision: float32 [48], replicated, may hold values from 1 to 4
Outputs:
- positions_out: float32 [16, 3, 65536], P('rep', None, 'sp')
- velocities_out: float32 [16, 3, 65536], P('rep', None, 'sp')
Inputs may be any that keep to these rules, and one draw needn't show every extreme that they name: `tile_lists`: for each replica, step and local block b of a domain (numbered 0 to 63), the 4 entries are distinct extended block numbers from b to b + 64, among them b, b + 32 and b + 64. `solute_index`: within each replica and domain the 256 entries are distinct local atom numbers.
All inputs are finite; a program needn't handle non-finite values.
Results may differ from a plain program's by a relative error of at most 0.0001.
Values sent between devices are 32-bit elements; how exact they have to be, the bound alone decides.
No kernel may reach another device: no remote copies, remote signals or barrier semaphores. Data moves between devices by JAX's collectives and lax.ppermute only.
A program may use at most 128 MiB of HBM per device.

v0:
```python
import math
import jax
import jax.numpy as jnp
from jax import lax
from jax.sharding import PartitionSpec as P

M = 784
OUTER = 2
INNER = 2
TIME_STEP = 0.05
PAIR_STRENGTH = 0.2
HALF_INVERSE = 0.03125
shell_batch = 8
group_limit = 8


def extended_2(cells, sides, width):
    for axis, dim in sides:
        count = lax.axis_size(axis)
        ends = count - 1
        head = lax.slice_in_dim(cells, 0, width, axis=dim)
        tail = lax.slice_in_dim(cells, cells.shape[dim] - width, cells.shape[dim], axis=dim)
        cells = jnp.concatenate(
            [
                lax.ppermute(tail, axis, [(i, (i + 1) % count) for i in range(ends)]),
                cells,
                lax.ppermute(head, axis, [((i + 1) % count, i) for i in range(ends)]),
            ],
            axis=dim,
        )
    return cells


def directions(total_terms):
    order_index = jnp.arange(total_terms, dtype=jnp.int32)
    height = 1.0 - (2.0 * order_index.astype(jnp.float32) + 1.0) / total_terms
    radius = jnp.sqrt(1.0 - height * height)
    azimuth = (order_index * 610 % 987).astype(jnp.float32) * (2.0 * math.pi / 987.0)
    return (radius * jnp.cos(azimuth), radius * jnp.sin(azimuth), height)


def shell_values(total_shells):
    return 1.0 + 3.0 * jnp.arange(total_shells, dtype=jnp.int32).astype(jnp.float32) / total_shells


def projection(points, dir_x, dir_y, dir_z):
    return (
        dir_x[:, None] * points[0][None, :]
        + dir_y[:, None] * points[1][None, :]
        + dir_z[:, None] * points[2][None, :]
    )


def amplitude_terms(project, weights, shell_q):
    shell_blocks = shell_q.reshape(-1, shell_batch)

    def one_block(shell_block):
        phases = shell_block[:, None, None] * project[None]
        return jnp.stack(
            [
                jnp.sum(weights * jnp.cos(phases), axis=-1),
                jnp.sum(weights * jnp.sin(phases), axis=-1),
            ]
        )

    result = lax.map(one_block, shell_blocks)
    return jnp.transpose(result, (1, 0, 2, 3)).reshape(2, -1, project.shape[0])


def shell_intensity(amplitude):
    return jnp.mean(amplitude[0] * amplitude[0] + amplitude[1] * amplitude[1], axis=-1)


def scale_grad(amplitude, intensity, precision, intensity_exp, total_terms):
    coef_shell = 2.0 * precision * (intensity - intensity_exp) / total_terms
    return coef_shell[None, :, None] * amplitude


def restraint_forces(project, weights, shell_q, weight_grad, dir_x, dir_y, dir_z):
    shell_blocks = shell_q.reshape(-1, shell_batch)
    grad_real = weight_grad[0].reshape(-1, shell_batch, project.shape[0])
    grad_imag = weight_grad[1].reshape(-1, shell_batch, project.shape[0])

    def add_block(running, pieces):
        shell_block, block_real, block_imag = pieces
        phases = shell_block[:, None, None] * project[None]
        block_term = jnp.sum(
            shell_block[:, None, None]
            * (block_imag[:, :, None] * jnp.cos(phases) - block_real[:, :, None] * jnp.sin(phases)),
            axis=0,
        )
        return (running + block_term, None)

    running, unused = lax.scan(
        add_block, jnp.zeros(project.shape, jnp.float32), (shell_blocks, grad_real, grad_imag)
    )
    return jnp.stack(
        [
            -weights * jnp.sum(dir_x[:, None] * running, axis=0),
            -weights * jnp.sum(dir_y[:, None] * running, axis=0),
            -weights * jnp.sum(dir_z[:, None] * running, axis=0),
        ]
    )


def pair_group(own_rows, near_rows, coupling):
    delta_list = [
        own_rows[component][:, :, None] - near_rows[component][:, None, :] for component in range(3)
    ]
    distance = (
        delta_list[0] * delta_list[0]
        + delta_list[1] * delta_list[1]
        + delta_list[2] * delta_list[2]
    )
    pair_weight = (
        coupling
        * own_rows[3][:, :, None]
        * near_rows[3][:, None, :]
        * jnp.exp(-HALF_INVERSE * distance)
    )
    return jnp.stack([jnp.sum(pair_weight * delta, axis=-1) for delta in delta_list])


def pair_forces(own_blocks, ext_blocks, tile_list):
    block_count, neighbours = tile_list.shape
    block_width = own_blocks.shape[2]
    group_size = min(group_limit, block_count)
    coupling = PAIR_STRENGTH / math.sqrt(neighbours * block_width)
    nearby = jnp.take(ext_blocks, tile_list.reshape(-1), axis=1).reshape(
        4, block_count // group_size, group_size, neighbours * block_width
    )
    grouped = own_blocks.reshape(4, block_count // group_size, group_size, block_width)

    def one_group(pieces):
        return pair_group(pieces[0], pieces[1], coupling)

    result = lax.map(one_group, (jnp.moveaxis(grouped, 1, 0), jnp.moveaxis(nearby, 1, 0)))
    return jnp.moveaxis(result, 0, 1).reshape(3, -1)


def shards(
    positions,
    velocities,
    strength,
    inv_mass,
    tile_lists,
    solute_index,
    scatter_weight,
    intensity_exp,
    precision,
):
    coords_now = positions[0]
    speed_now = velocities[0]
    charge = strength[0]
    inverse = inv_mass[0]
    solute_slots = solute_index[0]
    weights = scatter_weight[0]
    atom_dev = coords_now.shape[1]
    rim_width = atom_dev // 2
    block_width = 128
    replica_count = lax.axis_size("rep")
    scale_norm = 1.0 / math.sqrt(lax.axis_size("sp") * solute_slots.shape[0])
    dir_x, dir_y, dir_z = directions(M)
    shell_q = shell_values(intensity_exp.shape[0])
    mass_here = inverse[solute_slots]
    for outer_step in range(OUTER):
        points = jnp.take(coords_now, solute_slots, axis=1)
        project = projection(points, dir_x, dir_y, dir_z)
        partial_value = amplitude_terms(project, weights, shell_q) * scale_norm
        amplitude = lax.psum(partial_value, "sp")
        intensity = lax.psum(shell_intensity(amplitude), "rep") / replica_count
        weight_grad = scale_grad(amplitude, intensity, precision, intensity_exp, M)
        saxs_kick = restraint_forces(project, weights, shell_q, weight_grad, dir_x, dir_y, dir_z)
        for inner_step in range(INNER):
            tile_list = tile_lists[0, outer_step * INNER + inner_step]
            rows_all = jnp.concatenate([coords_now, charge[None, :]], axis=0)
            extended = extended_2(rows_all, (("sp", 1),), rim_width)
            own_blocks = rows_all.reshape(4, atom_dev // block_width, block_width)
            ext_blocks = extended.reshape(4, extended.shape[1] // block_width, block_width)
            pair_push = pair_forces(own_blocks, ext_blocks, tile_list)
            speed_now = speed_now + TIME_STEP * inverse[None, :] * pair_push
            coords_now = coords_now + TIME_STEP * speed_now
        impulse = INNER * TIME_STEP * mass_here[None, :] * saxs_kick
        speed_now = speed_now.at[:, solute_slots].add(impulse)
    return (coords_now[None], speed_now[None])


def solution(mesh):
    in_specs = (
        P("rep", None, "sp"),
        P("rep", None, "sp"),
        P("rep", "sp"),
        P("rep", "sp"),
        P("rep", None, "sp", None),
        P("rep", "sp"),
        P("rep", "sp"),
        P(),
        P(),
    )
    out_specs = (P("rep", None, "sp"), P("rep", None, "sp"))
    return jax.shard_map(shards, mesh=mesh, in_specs=in_specs, out_specs=out_specs, check_vma=False)
```

profile of v0, /device:TPU:24, one launch (start us, length us, event | category | flops | bytes accessed | tf_op | source)
XLA Modules:
  0.0 899.1 jit_solution(11121404440708950667)
XLA Ops:
  7.3 3.4 copy.163
  10.7 2.9 copy.166
  13.6 3.5 collective-permute-start
  17.1 2.4 collective-permute-start.1
  20.7 2.6 copy.164
  23.3 2.9 gather_fusion.4
  29.6 16.2 %while.84 = (s32[]{:T(128)}, f32[8,3,8,128]{3,2,1,0:T(8,128)S(1)}, f32[8,4,8,128]{3,2,0,1:T(8,128)S(1)}, f32[8,4,8,512]{3,2,0,1:T(8,128)S(1)}, s32[]{:T(128)}) while((s32[]{:T(128)}, f32[8,3,8,128]{3,2,1,0:T(8,128)S(1)}, f32[8,4,8,128]{3,2,0,1:T(8,128)S(1)}, f32[8,4,8,512]{3,2,0,1:T(8,128)S(1)}, s32[]{:T(128)}) %tuple.295), condition=%wide.region_4.6_spmd, body=%wide.region_0.5_spmd.sunk | while | flops 8916994 | bytes 446537 | solution.py:137
  45.9 2.7 copy.171
  48.5 7.0 multiply_add_fusion.6
  55.5 2.8 copy.172
  58.5 5.6 collective-permute-start.2
  64.1 2.4 collective-permute-start.3
  66.6 5.8 collective-permute-done.3
  74.0 16.2 %while.85 = (s32[]{:T(128)}, f32[8,3,8,128]{3,2,1,0:T(8,128)S(1)}, f32[8,4,8,128]{3,2,1,0:T(8,128)S(1)}, f32[8,4,8,512]{3,2,0,1:T(8,128)S(1)}, s32[]{:T(128)}, /*index=5*/s32[]{:T(128)}, s32[]{}, s32[]{}, s32[]{}) while((s32[]{:T(128)}, f32[8,3,8,128]{3,2,1,0:T(8,128)S(1)}, f32[8,4,8,128]{3,2,1,0:T(8,128)S(1)}, ...), condition=%wide.region_9.11_spmd, body=%wide.region_5.10_spmd.sunk | while | flops 8916997 | bytes 413849 | solution.py:137
  90.2 2.7 copy.178
  92.9 8.5 multiply_add_fusion.5
  101.4 2.9 gather_fusion.6
  104.3 2.8 copy.179
  107.9 150.7 %while.89 = (s32[]{:T(128)}, f32[6,2,8,784]{3,2,0,1:T(8,128)S(1)}, f32[1,256]{1,0:T(1,128)S(1)}, f32[6,8]{1,0:T(8,128)S(1)}, f32[256]{0:T(256)S(1)}, /*index=5*/...) while((s32[]{:T(128)}, f32[6,2,8,784]{3,2,0,1:T(8,128)S(1)}, ...), condition=%wide.region_37.40_spmd.clone, body=%wide.region_34.39_spmd.clone.sunk | while | flops 9031682 | bytes 1784213 | solution.py:66
  108.3 24.7 %fusion.158 = (f32[8,784]{1,0:T(8,128)S(1)}, f32[8,784]{1,0:T(8,128)S(1)}) fusion(f32[784,256]{1,0:T(8,128)S(1)} %multiply_add_fusion.13, f32[8]{0:T(128)S(1)} %fusion.157, f32[256]{0:T(256)S(1)} %bitcast.407), kind=kLoop, calls=%fused_computation.132.clone.1 | loop fusion | flops 8015616 | bytes 854048 | tf_op jit(solution)/shard_map/while/body/eval_jaxpr/reduce_sum | solution.py:61
  133.5 24.7 %fusion.158 = (f32[8,784]{1,0:T(8,128)S(1)}, f32[8,784]{1,0:T(8,128)S(1)}) fusion(f32[784,256]{1,0:T(8,128)S(1)} %multiply_add_fusion.13, f32[8]{0:T(128)S(1)} %fusion.157, f32[256]{0:T(256)S(1)} %bitcast.407), kind=kLoop, calls=%fused_computation.132.clone.1 | loop fusion | flops 8015616 | bytes 854048 | tf_op jit(solution)/shard_map/while/body/eval_jaxpr/reduce_sum | solution.py:61
  158.6 24.7 %fusion.158 = (f32[8,784]{1,0:T(8,128)S(1)}, f32[8,784]{1,0:T(8,128)S(1)}) fusion(f32[784,256]{1,0:T(8,128)S(1)} %multiply_add_fusion.13, f32[8]{0:T(128)S(1)} %fusion.157, f32[256]{0:T(256)S(1)} %bitcast.407), kind=kLoop, calls=%fused_computation.132.clone.1 | loop fusion | flops 8015616 | bytes 854048 | tf_op jit(solution)/shard_map/while/body/eval_jaxpr/reduce_sum | solution.py:61
  183.7 24.7 %fusion.158 = (f32[8,784]{1,0:T(8,128)S(1)}, f32[8,784]{1,0:T(8,128)S(1)}) fusion(f32[784,256]{1,0:T(8,128)S(1)} %multiply_add_fusion.13, f32[8]{0:T(128)S(1)} %fusion.157, f32[256]{0:T(256)S(1)} %bitcast.407), kind=kLoop, calls=%fused_computation.132.clone.1 | loop fusion | flops 8015616 | bytes 854048 | tf_op jit(solution)/shard_map/while/body/eval_jaxpr/reduce_sum | solution.py:61
  208.8 24.7 %fusion.158 = (f32[8,784]{1,0:T(8,128)S(1)}, f32[8,784]{1,0:T(8,128)S(1)}) fusion(f32[784,256]{1,0:T(8,128)S(1)} %multiply_add_fusion.13, f32[8]{0:T(128)S(1)} %fusion.157, f32[256]{0:T(256)S(1)} %bitcast.407), kind=kLoop, calls=%fused_computation.132.clone.1 | loop fusion | flops 8015616 | bytes 854048 | tf_op jit(solution)/shard_map/while/body/eval_jaxpr/reduce_sum | solution.py:61
  233.9 24.7 %fusion.158 = (f32[8,784]{1,0:T(8,128)S(1)}, f32[8,784]{1,0:T(8,128)S(1)}) fusion(f32[784,256]{1,0:T(8,128)S(1)} %multiply_add_fusion.13, f32[8]{0:T(128)S(1)} %fusion.157, f32[256]{0:T(256)S(1)} %bitcast.407), kind=kLoop, calls=%fused_computation.132.clone.1 | loop fusion | flops 8015616 | bytes 854048 | tf_op jit(solution)/shard_map/while/body/eval_jaxpr/reduce_sum | solution.py:61
  259.4 150.9 %while.88 = (s32[]{:T(128)}, f32[6,2,8,784]{3,2,0,1:T(8,128)S(1)}, f32[1,256]{1,0:T(1,128)S(1)}, f32[6,8]{1,0:T(8,128)S(1)}, f32[256]{0:T(256)S(1)}, /*index=5*/...) while((s32[]{:T(128)}, f32[6,2,8,784]{3,2,0,1:T(8,128)S(1)}, ...), condition=%wide.region_18.21_spmd.clone, body=%wide.region_15.20_spmd.clone.sunk | while | flops 9031682 | bytes 1784213 | solution.py:66
  260.0 24.7 %fusion.155 = (f32[8,784]{1,0:T(8,128)S(1)}, f32[8,784]{1,0:T(8,128)S(1)}) fusion(f32[784,256]{1,0:T(8,128)S(1)} %multiply_add_fusion.12, f32[8]{0:T(128)S(1)} %fusion.154, f32[256]{0:T(256)S(1)} %bitcast.408), kind=kLoop, calls=%fused_computation.121.clone.1 | loop fusion | flops 8015616 | bytes 854048 | tf_op jit(solution)/shard_map/while/body/eval_jaxpr/reduce_sum | solution.py:61
  285.1 24.7 %fusion.155 = (f32[8,784]{1,0:T(8,128)S(1)}, f32[8,784]{1,0:T(8,128)S(1)}) fusion(f32[784,256]{1,0:T(8,128)S(1)} %multiply_add_fusion.12, f32[8]{0:T(128)S(1)} %fusion.154, f32[256]{0:T(256)S(1)} %bitcast.408), kind=kLoop, calls=%fused_computation.121.clone.1 | loop fusion | flops 8015616 | bytes 854048 | tf_op jit(solution)/shard_map/while/body/eval_jaxpr/reduce_sum | solution.py:61
  310.2 24.7 %fusion.155 = (f32[8,784]{1,0:T(8,128)S(1)}, f32[8,784]{1,0:T(8,128)S(1)}) fusion(f32[784,256]{1,0:T(8,128)S(1)} %multiply_add_fusion.12, f32[8]{0:T(128)S(1)} %fusion.154, f32[256]{0:T(256)S(1)} %bitcast.408), kind=kLoop, calls=%fused_computation.121.clone.1 | loop fusion | flops 8015616 | bytes 854048 | tf_op jit(solution)/shard_map/while/body/eval_jaxpr/reduce_sum | solution.py:61
  335.4 24.7 %fusion.155 = (f32[8,784]{1,0:T(8,128)S(1)}, f32[8,784]{1,0:T(8,128)S(1)}) fusion(f32[784,256]{1,0:T(8,128)S(1)} %multiply_add_fusion.12, f32[8]{0:T(128)S(1)} %fusion.154, f32[256]{0:T(256)S(1)} %bitcast.408), kind=kLoop, calls=%fused_computation.121.clone.1 | loop fusion | flops 8015616 | bytes 854048 | tf_op jit(solution)/shard_map/while/body/eval_jaxpr/reduce_sum | solution.py:61
  360.5 24.7 %fusion.155 = (f32[8,784]{1,0:T(8,128)S(1)}, f32[8,784]{1,0:T(8,128)S(1)}) fusion(f32[784,256]{1,0:T(8,128)S(1)} %multiply_add_fusion.12, f32[8]{0:T(128)S(1)} %fusion.154, f32[256]{0:T(256)S(1)} %bitcast.408), kind=kLoop, calls=%fused_computation.121.clone.1 | loop fusion | flops 8015616 | bytes 854048 | tf_op jit(solution)/shard_map/while/body/eval_jaxpr/reduce_sum | solution.py:61
  385.6 24.7 %fusion.155 = (f32[8,784]{1,0:T(8,128)S(1)}, f32[8,784]{1,0:T(8,128)S(1)}) fusion(f32[784,256]{1,0:T(8,128)S(1)} %multiply_add_fusion.12, f32[8]{0:T(128)S(1)} %fusion.154, f32[256]{0:T(256)S(1)} %bitcast.408), kind=kLoop, calls=%fused_computation.121.clone.1 | loop fusion | flops 8015616 | bytes 854048 | tf_op jit(solution)/shard_map/while/body/eval_jaxpr/reduce_sum | solution.py:61
  413.0 3.9 collective-permute-start.5
  417.2 4.0 collective-permute-done.5
  422.8 16.2 %while.86 = (s32[]{:T(128)}, f32[8,3,8,128]{3,2,1,0:T(8,128)S(1)}, f32[8,4,8,128]{3,2,1,0:T(8,128)S(1)}, f32[8,4,8,512]{3,2,0,1:T(8,128)S(1)}, s32[]{:T(128)}, /*index=5*/s32[]{:T(128)}, s32[]{}, s32[]{}, s32[]{}) while((s32[]{:T(128)}, f32[8,3,8,128]{3,2,1,0:T(8,128)S(1)}, f32[8,4,8,128]{3,2,1,0:T(8,128)S(1)}, ...), condition=%wide.region_14.16_spmd, body=%wide.region_10.15_spmd.sunk | while | flops 8916997 | bytes 413849 | solution.py:137
  439.0 2.7 copy.185
  441.7 8.7 fusion.73
  450.4 42.0 %all-reduce.4.cloned.1.call-done = (f32[2,48,784]{2,1,0:T(8,128)}, f32[2,48,784]{2,1,0:T(8,128)}) async-done(((f32[2,48,784]{2,1,0:T(8,128)}, f32[2,48,784]{2,1,0:T(8,128)}), (f32[2,48,784]{2,1,0:T(8,128)}, f32[2,48,784]{2,1,0:T(8,128)})) %all-reduce.4.cloned.1.call-update) | async-done | bytes 602128 | tf_op jit(solution)/shard_map/psum | solution.py:170
  494.7 33.4 %all-reduce = (f32[48]{0:T(128)S(1)}, f32[48]{0:T(128)S(1)}) all-reduce(f32[48]{0:T(128)S(1)} %broadcast_multiply_fusion.5, f32[48]{0:T(128)S(1)} %broadcast_multiply_fusion.4), channel_id=1, replica_groups=mesh['rep'=16,'sp'=8] {'rep'}, use_global_device_ids=true, to_apply=%region_21.24 | all-reduce | flops 96 | bytes 768 | tf_op jit(solution)/shard_map/psum | solution.py:171
  529.2 146.9 %while.91 = (s32[]{:T(128)}, f32[784,256]{1,0:T(8,128)S(1)}, f32[6,8]{1,0:T(8,128)S(1)}, f32[6,8,784]{2,1,0:T(8,128)S(1)}, f32[6,8,784]{2,1,0:T(8,128)S(1)}, /*i...) while((s32[]{:T(128)}, f32[784,256]{1,0:T(8,128)S(1)}, ...), condition=%wide.region_43.46_spmd.clone, body=%wide.region_41.45_spmd.clone.sunk | while | flops 10838019 | bytes 4980143 | solution.py:94
  529.6 23.8 %fusion.163 = f32[784,256]{1,0:T(8,128)S(1)} fusion(f32[8,784]{1,0:T(8,128)S(1)} %get-tuple-element.1134, f32[784,256]{1,0:T(8,128)S(1)} %multiply_add_fusion.15, f32[8,784]{1,0:T(8,128)S(1)} %get-tuple-element.1135, f32[8]{0:T(128)S(1)} %fusion.162), kind=kLoop, calls=%fused_computation.158.clone.1 | loop fusion | flops 9433088 | bytes 1655840 | tf_op jit(solution)/shard_map/while/body/eval_jaxpr/reduce_sum | solution.py:87
  554.1 23.8 %fusion.163 = f32[784,256]{1,0:T(8,128)S(1)} fusion(f32[8,784]{1,0:T(8,128)S(1)} %get-tuple-element.1134, f32[784,256]{1,0:T(8,128)S(1)} %multiply_add_fusion.15, f32[8,784]{1,0:T(8,128)S(1)} %get-tuple-element.1135, f32[8]{0:T(128)S(1)} %fusion.162), kind=kLoop, calls=%fused_computation.158.clone.1 | loop fusion | flops 9433088 | bytes 1655840 | tf_op jit(solution)/shard_map/while/body/eval_jaxpr/reduce_sum | solution.py:87
  578.6 23.8 %fusion.163 = f32[784,256]{1,0:T(8,128)S(1)} fusion(f32[8,784]{1,0:T(8,128)S(1)} %get-tuple-element.1134, f32[784,256]{1,0:T(8,128)S(1)} %multiply_add_fusion.15, f32[8,784]{1,0:T(8,128)S(1)} %get-tuple-element.1135, f32[8]{0:T(128)S(1)} %fusion.162), kind=kLoop, calls=%fused_computation.158.clone.1 | loop fusion | flops 9433088 | bytes 1655840 | tf_op jit(solution)/shard_map/while/body/eval_jaxpr/reduce_sum | solution.py:87
  603.1 23.8 %fusion.163 = f32[784,256]{1,0:T(8,128)S(1)} fusion(f32[8,784]{1,0:T(8,128)S(1)} %get-tuple-element.1134, f32[784,256]{1,0:T(8,128)S(1)} %multiply_add_fusion.15, f32[8,784]{1,0:T(8,128)S(1)} %get-tuple-element.1135, f32[8]{0:T(128)S(1)} %fusion.162), kind=kLoop, calls=%fused_computation.158.clone.1 | loop fusion | flops 9433088 | bytes 1655840 | tf_op jit(solution)/shard_map/while/body/eval_jaxpr/reduce_sum | solution.py:87
  627.5 23.8 %fusion.163 = f32[784,256]{1,0:T(8,128)S(1)} fusion(f32[8,784]{1,0:T(8,128)S(1)} %get-tuple-element.1134, f32[784,256]{1,0:T(8,128)S(1)} %multiply_add_fusion.15, f32[8,784]{1,0:T(8,128)S(1)} %get-tuple-element.1135, f32[8]{0:T(128)S(1)} %fusion.162), kind=kLoop, calls=%fused_computation.158.clone.1 | loop fusion | flops 9433088 | bytes 1655840 | tf_op jit(solution)/shard_map/while/body/eval_jaxpr/reduce_sum | solution.py:87
  652.0 23.8 %fusion.163 = f32[784,256]{1,0:T(8,128)S(1)} fusion(f32[8,784]{1,0:T(8,128)S(1)} %get-tuple-element.1134, f32[784,256]{1,0:T(8,128)S(1)} %multiply_add_fusion.15, f32[8,784]{1,0:T(8,128)S(1)} %get-tuple-element.1135, f32[8]{0:T(128)S(1)} %fusion.162), kind=kLoop, calls=%fused_computation.158.clone.1 | loop fusion | flops 9433088 | bytes 1655840 | tf_op jit(solution)/shard_map/while/body/eval_jaxpr/reduce_sum | solution.py:87
  676.2 146.9 %while.90 = (s32[]{:T(128)}, f32[784,256]{1,0:T(8,128)S(1)}, f32[6,8]{1,0:T(8,128)S(1)}, f32[6,8,784]{2,1,0:T(8,128)S(1)}, f32[6,8,784]{2,1,0:T(8,128)S(1)}, /*i...) while((s32[]{:T(128)}, f32[784,256]{1,0:T(8,128)S(1)}, ...), condition=%wide.region_24.27_spmd.clone, body=%wide.region_22.26_spmd.clone.sunk | while | flops 10838019 | bytes 4980143 | solution.py:94
  676.6 23.8 %fusion.161 = f32[784,256]{1,0:T(8,128)S(1)} fusion(f32[8,784]{1,0:T(8,128)S(1)} %get-tuple-element.1121, f32[784,256]{1,0:T(8,128)S(1)} %multiply_add_fusion.14, f32[8,784]{1,0:T(8,128)S(1)} %get-tuple-element.1122, f32[8]{0:T(128)S(1)} %fusion.160), kind=kLoop, calls=%fused_computation.145.clone.1 | loop fusion | flops 9433088 | bytes 1655840 | tf_op jit(solution)/shard_map/while/body/eval_jaxpr/reduce_sum | solution.py:87
  701.1 23.8 %fusion.161 = f32[784,256]{1,0:T(8,128)S(1)} fusion(f32[8,784]{1,0:T(8,128)S(1)} %get-tuple-element.1121, f32[784,256]{1,0:T(8,128)S(1)} %multiply_add_fusion.14, f32[8,784]{1,0:T(8,128)S(1)} %get-tuple-element.1122, f32[8]{0:T(128)S(1)} %fusion.160), kind=kLoop, calls=%fused_computation.145.clone.1 | loop fusion | flops 9433088 | bytes 1655840 | tf_op jit(solution)/shard_map/while/body/eval_jaxpr/reduce_sum | solution.py:87
  725.6 23.8 %fusion.161 = f32[784,256]{1,0:T(8,128)S(1)} fusion(f32[8,784]{1,0:T(8,128)S(1)} %get-tuple-element.1121, f32[784,256]{1,0:T(8,128)S(1)} %multiply_add_fusion.14, f32[8,784]{1,0:T(8,128)S(1)} %get-tuple-element.1122, f32[8]{0:T(128)S(1)} %fusion.160), kind=kLoop, calls=%fused_computation.145.clone.1 | loop fusion | flops 9433088 | bytes 1655840 | tf_op jit(solution)/shard_map/while/body/eval_jaxpr/reduce_sum | solution.py:87
  750.1 23.8 %fusion.161 = f32[784,256]{1,0:T(8,128)S(1)} fusion(f32[8,784]{1,0:T(8,128)S(1)} %get-tuple-element.1121, f32[784,256]{1,0:T(8,128)S(1)} %multiply_add_fusion.14, f32[8,784]{1,0:T(8,128)S(1)} %get-tuple-element.1122, f32[8]{0:T(128)S(1)} %fusion.160), kind=kLoop, calls=%fused_computation.145.clone.1 | loop fusion | flops 9433088 | bytes 1655840 | tf_op jit(solution)/shard_map/while/body/eval_jaxpr/reduce_sum | solution.py:87
  774.6 23.8 %fusion.161 = f32[784,256]{1,0:T(8,128)S(1)} fusion(f32[8,784]{1,0:T(8,128)S(1)} %get-tuple-element.1121, f32[784,256]{1,0:T(8,128)S(1)} %multiply_add_fusion.14, f32[8,784]{1,0:T(8,128)S(1)} %get-tuple-element.1122, f32[8]{0:T(128)S(1)} %fusion.160), kind=kLoop, calls=%fused_computation.145.clone.1 | loop fusion | flops 9433088 | bytes 1655840 | tf_op jit(solution)/shard_map/while/body/eval_jaxpr/reduce_sum | solution.py:87
  799.0 23.8 %fusion.161 = f32[784,256]{1,0:T(8,128)S(1)} fusion(f32[8,784]{1,0:T(8,128)S(1)} %get-tuple-element.1121, f32[784,256]{1,0:T(8,128)S(1)} %multiply_add_fusion.14, f32[8,784]{1,0:T(8,128)S(1)} %get-tuple-element.1122, f32[8]{0:T(128)S(1)} %fusion.160), kind=kLoop, calls=%fused_computation.145.clone.1 | loop fusion | flops 9433088 | bytes 1655840 | tf_op jit(solution)/shard_map/while/body/eval_jaxpr/reduce_sum | solution.py:87
  823.7 5.9 scatter_fusion
  829.6 5.9 multiply_add_fusion.4
  835.4 2.8 copy.188
  838.4 4.4 collective-permute-start.6
  845.1 5.9 collective-permute-done.7
  852.7 16.2 %while.87 = (s32[]{:T(128)}, f32[8,3,8,128]{3,2,1,0:T(8,128)S(1)}, f32[8,4,8,128]{3,2,1,0:T(8,128)S(1)}, f32[8,4,8,512]{3,2,0,1:T(8,128)S(1)}, s32[]{:T(128)}, /*index=5*/s32[]{:T(128)}, s32[]{}, s32[]{}, s32[]{}) while((s32[]{:T(128)}, f32[8,3,8,128]{3,2,1,0:T(8,128)S(1)}, f32[8,4,8,128]{3,2,1,0:T(8,128)S(1)}, ...), condition=%wide.region_33.36_spmd, body=%wide.region_29.35_spmd.sunk | while | flops 8916997 | bytes 413849 | solution.py:137
  868.9 2.7 copy.193
  871.6 7.7 add_bitcast_fusion
  879.2 5.9 scatter_fusion.1
  885.1 3.5 copy.197
  888.6 3.5 copy.196
  (370 shorter events, 95.5 us)
Async XLA Ops:
  7.2 6.4 copy-start.1
  7.2 12.3 %copy-start.5 = (s32[1,4,64,4]{2,3,1,0:T(4,128)S(1)}, s32[1,4,64,4]{2,3,1,0:T(4,128)}, u32[]{:S(2)}) copy-start(s32[1,4,64,4]{2,3,1,0:T(4,128)} %param.33) | copy-start | bytes 12292
  7.2 12.8 %copy-start.6 = (s32[1,256]{1,0:T(1,128)S(1)}, s32[1,256]{1,0:T(1,128)}, u32[]{:S(2)}) copy-start(s32[1,256]{1,0:T(1,128)} %param.34) | copy-start | bytes 3076
  7.2 13.4 %copy-start = (f32[1,8192]{1,0:T(1,128)S(1)}, f32[1,8192]{1,0:T(1,128)}, u32[]{:S(2)}) copy-start(f32[1,8192]{1,0:T(1,128)} %param.32) | copy-start | bytes 98308
  7.2 13.5 %copy-start.4 = (f32[1,3,8192]{2,0,1:T(1,128)S(1)}, f32[1,3,8192]{2,0,1:T(1,128)}, u32[]{:S(2)}) copy-start(f32[1,3,8192]{2,0,1:T(1,128)} %param.30) | copy-start | bytes 294916
  7.2 485.2 %all-reduce.4.cloned.1.call-start = ((), (), s32[]{:S(2)}) async-start(), calls=%async_computation | async-start | bytes 1376256 | tf_op jit(solution)/shard_map/psum | solution.py:170
  10.7 17.3 %copy-start.3 = (f32[1,3,8192]{2,0,1:T(1,128)S(1)}, f32[1,3,8192]{2,0,1:T(1,128)}, u32[]{:S(2)}) copy-start(f32[1,3,8192]{2,0,1:T(1,128)} %param.29) | copy-start | bytes 294916
  13.6 14.4 %collective-permute-start = (f32[4,4096]{1,0:T(4,128)S(1)}, f32[4,4096]{1,0:T(4,128)S(1)}, u32[]{:S(2)}, u32[]{:S(2)}) collective-permute-start(f32[4,4096]{1,0:T(4,128)S(1)} %get-tuple-element.653), channel_id=1, source_target_pairs={{0,1},{1,2},{2,3},{3,4},{4,5},{5,6},{6,7},{8,9},{9,10},{10,11},{11... | collective-permute-start | bytes 196616 | tf_op jit(solution)/shard_map/ppermute | solution.py:25
  17.1 10.9 %collective-permute-start.1 = (f32[4,4096]{1,0:T(4,128)S(1)}, f32[4,4096]{1,0:T(4,128)S(1)}, u32[]{:S(2)}, u32[]{:S(2)}) collective-permute-start(f32[4,4096]{1,0:T(4,128)S(1)} %get-tuple-element.654), channel_id=1, source_target_pairs={{1,0},{2,1},{3,2},{4,3},{5,4},{6,5},{7,6},{9,8},{10,9},{11,10},{12... | collective-permute-start | bytes 196616 | tf_op jit(solution)/shard_map/ppermute | solution.py:27
  58.5 8.1 collective-permute-start.2
  64.1 8.3 collective-permute-start.3
  101.4 6.5 copy-start.7
  411.1 6.1 collective-permute-start.4
  413.0 8.3 collective-permute-start.5
  441.7 86.4 %copy-start.8 = (f32[48]{0:T(128)S(1)}, f32[48]{0:T(128)}, u32[]{:S(2)}) copy-start(f32[48]{0:T(128)} %param.36) | copy-start | bytes 580
  441.7 86.4 %copy-start.9 = (f32[48]{0:T(128)S(1)}, f32[48]{0:T(128)}, u32[]{:S(2)}) copy-start(f32[48]{0:T(128)} %param.37) | copy-start | bytes 580
  529.2 146.9 %copy-start.2 = (f32[2,48,784]{2,1,0:T(8,128)S(1)}, f32[2,48,784]{2,1,0:T(8,128)}, u32[]{:S(2)}) copy-start(f32[2,48,784]{2,1,0:T(8,128)} %get-tuple-element.603) | copy-start | bytes 903172
  838.4 6.7 collective-permute-start.6
  842.8 8.3 collective-permute-start.7
Sparse Core Ops, SparseCore 0:
  417.1 75.2 all-reduce.3
where the time goes:
time: 904 us; the launch traced here: 899 us
  other arithmetic  713 us (79%)
  waiting for transfers between devices  58.1 us (6%)
  local copies, waits for them, and re-layouts  49.9 us (6%)
  blocking collectives  33.4 us (4%)
  starting transfers between devices  26.3 us (3%)
  between operations  15.1 us (2%)
    reduce_sum x12, other arithmetic, one_block(): jnp.sum(weights * jnp.cos(phases), axis=-1)  296 us
    reduce_sum x12, other arithmetic, add_block(): jnp.sum(shell_block[:, None, None] * (block_imag[:, :, None] * jnp.cos(ph...  286 us
    reduce_sum x32, other arithmetic, pair_group(): jnp.sum(pair_weight * delta, axis=-1)  61.6 us
    psum x1, waiting for transfers between devices, shards(): amplitude = lax.psum(partial_value, 'sp')  42 us
    psum x1, blocking collectives, shards(): intensity = lax.psum(shell_intensity(amplitude), 'rep') / replica_count  33.4 us
    add x3, other arithmetic, shards(): coords_now = coords_now + TIME_STEP * speed_now  21.4 us
  transfers between devices with their start and end apart: 9, of which 5 were waited for; matrix products, arithmetic and copies ran while one was open for 4% of the time, Pallas kernels for 0%

commit v1 on v0

--- a/solution.py
+++ b/solution.py
@@ -167,7 +167,8 @@
         points = jnp.take(coords_now, solute_slots, axis=1)
         project = projection(points, dir_x, dir_y, dir_z)
         partial_value = amplitude_terms(project, weights, shell_q) * scale_norm
-        amplitude = lax.psum(partial_value, "sp")
+        blocks = lax.all_gather(partial_value, "sp")
+        amplitude = jnp.sum(blocks, axis=0)
         intensity = lax.psum(shell_intensity(amplitude), "rep") / replica_count
         weight_grad = scale_grad(amplitude, intensity, precision, intensity_exp, M)
         saxs_kick = restraint_forces(project, weights, shell_q, weight_grad, dir_x, dir_y, dir_z)

time: 904 us -> 872 us (0.965)
  waiting for transfers between devices: 58.1 us -> 23.2 us
    psum x1 -> x0, waiting for transfers between devices: 42 us -> none  [shards(): amplitude = lax.psum(partial_value, 'sp')]
    all_gather x0 -> x2, waiting for transfers between devices: none -> 11.4 us  [shards(): blocks = lax.all_gather(partial_value, 'sp')]
  transfers between devices with their start and end apart: 9 -> 10, of which waited for: 5 -> 3; matrix products, arithmetic and copies ran while one was open for 4% -> 22% of each run, Pallas kernels for 0% -> 0%
where the time goes in v1:
time: 872 us; the launch traced here: 867 us
  other arithmetic  714 us (82%)
  local copies, waits for them, and re-layouts  50.6 us (6%)
  blocking collectives  34.5 us (4%)
  starting transfers between devices  26.1 us (3%)
  waiting for transfers between devices  23.2 us (3%)
  between operations  15.1 us (2%)
    reduce_sum x12, other arithmetic, one_block(): jnp.sum(weights * jnp.cos(phases), axis=-1)  296 us
    reduce_sum x12, other arithmetic, add_block(): jnp.sum(shell_block[:, None, None] * (block_imag[:, :, None] * jnp.cos(ph...  286 us
    reduce_sum x32, other arithmetic, pair_group(): jnp.sum(pair_weight * delta, axis=-1)  61.7 us
    psum x1, blocking collectives, shards(): intensity = lax.psum(shell_intensity(amplitude), 'rep') / replica_count  34.5 us
    add x3, other arithmetic, shards(): coords_now = coords_now + TIME_STEP * speed_now  21.4 us
  transfers between devices with their start and end apart: 10, of which 3 were waited for; matrix products, arithmetic and copies ran while one was open for 22% of the time, Pallas kernels for 0%

profile of v1, /device:TPU:24, one launch (start us, length us, event | category | flops | bytes accessed | tf_op | source)
XLA Modules:
  0.0 866.7 jit_solution(3918767461867138497)
XLA Ops:
  7.3 3.4 copy.163
  10.7 2.9 copy.166
  13.6 3.5 collective-permute-start
  17.1 2.4 collective-permute-start.1
  20.7 2.6 copy.164
  23.3 3.5 gather_fusion.4
  30.3 16.2 %while.84 = (s32[]{:T(128)}, f32[8,3,8,128]{3,2,1,0:T(8,128)S(1)}, f32[8,4,8,128]{3,2,0,1:T(8,128)S(1)}, f32[8,4,8,512]{3,2,0,1:T(8,128)S(1)}, s32[]{:T(128)}) while((s32[]{:T(128)}, f32[8,3,8,128]{3,2,1,0:T(8,128)S(1)}, f32[8,4,8,128]{3,2,0,1:T(8,128)S(1)}, f32[8,4,8,512]{3,2,0,1:T(8,128)S(1)}, s32[]{:T(128)}) %tuple.296), condition=%wide.region_4.6_spmd, body=%wide.region_0.5_spmd.sunk | while | flops 8916994 | bytes 446537 | solution.py:137
  46.5 2.7 copy.171
  49.2 7.0 multiply_add_fusion.6
  56.1 2.8 copy.172
  59.1 5.6 collective-permute-start.2
  64.7 2.4 collective-permute-start.3
  67.2 5.8 collective-permute-done.3
  74.6 16.2 %while.85 = (s32[]{:T(128)}, f32[8,3,8,128]{3,2,1,0:T(8,128)S(1)}, f32[8,4,8,128]{3,2,1,0:T(8,128)S(1)}, f32[8,4,8,512]{3,2,0,1:T(8,128)S(1)}, s32[]{:T(128)}, /*index=5*/s32[]{:T(128)}, s32[]{}, s32[]{}, s32[]{}) while((s32[]{:T(128)}, f32[8,3,8,128]{3,2,1,0:T(8,128)S(1)}, f32[8,4,8,128]{3,2,1,0:T(8,128)S(1)}, ...), condition=%wide.region_9.11_spmd, body=%wide.region_5.10_spmd.sunk | while | flops 8916997 | bytes 413849 | solution.py:137
  90.8 2.7 copy.178
  93.5 8.5 multiply_add_fusion.5
  102.0 2.9 gather_fusion.6
  105.0 2.8 copy.179
  108.6 150.7 %while.89 = (s32[]{:T(128)}, f32[6,2,8,784]{3,2,0,1:T(8,128)S(1)}, f32[1,256]{1,0:T(1,128)S(1)}, f32[6,8]{1,0:T(8,128)S(1)}, f32[256]{0:T(256)S(1)}, /*index=5*/...) while((s32[]{:T(128)}, f32[6,2,8,784]{3,2,0,1:T(8,128)S(1)}, ...), condition=%wide.region_37.40_spmd.clone, body=%wide.region_34.39_spmd.clone.sunk | while | flops 9031682 | bytes 1784213 | solution.py:66
  109.0 24.7 %fusion.158 = (f32[8,784]{1,0:T(8,128)S(1)}, f32[8,784]{1,0:T(8,128)S(1)}) fusion(f32[784,256]{1,0:T(8,128)S(1)} %multiply_add_fusion.13, f32[8]{0:T(128)S(1)} %fusion.157, f32[256]{0:T(256)S(1)} %bitcast.407), kind=kLoop, calls=%fused_computation.132.clone.1 | loop fusion | flops 8015616 | bytes 854048 | tf_op jit(solution)/shard_map/while/body/eval_jaxpr/reduce_sum | solution.py:61
  134.1 24.7 %fusion.158 = (f32[8,784]{1,0:T(8,128)S(1)}, f32[8,784]{1,0:T(8,128)S(1)}) fusion(f32[784,256]{1,0:T(8,128)S(1)} %multiply_add_fusion.13, f32[8]{0:T(128)S(1)} %fusion.157, f32[256]{0:T(256)S(1)} %bitcast.407), kind=kLoop, calls=%fused_computation.132.clone.1 | loop fusion | flops 8015616 | bytes 854048 | tf_op jit(solution)/shard_map/while/body/eval_jaxpr/reduce_sum | solution.py:61
  159.2 24.7 %fusion.158 = (f32[8,784]{1,0:T(8,128)S(1)}, f32[8,784]{1,0:T(8,128)S(1)}) fusion(f32[784,256]{1,0:T(8,128)S(1)} %multiply_add_fusion.13, f32[8]{0:T(128)S(1)} %fusion.157, f32[256]{0:T(256)S(1)} %bitcast.407), kind=kLoop, calls=%fused_computation.132.clone.1 | loop fusion | flops 8015616 | bytes 854048 | tf_op jit(solution)/shard_map/while/body/eval_jaxpr/reduce_sum | solution.py:61
  184.3 24.7 %fusion.158 = (f32[8,784]{1,0:T(8,128)S(1)}, f32[8,784]{1,0:T(8,128)S(1)}) fusion(f32[784,256]{1,0:T(8,128)S(1)} %multiply_add_fusion.13, f32[8]{0:T(128)S(1)} %fusion.157, f32[256]{0:T(256)S(1)} %bitcast.407), kind=kLoop, calls=%fused_computation.132.clone.1 | loop fusion | flops 8015616 | bytes 854048 | tf_op jit(solution)/shard_map/while/body/eval_jaxpr/reduce_sum | solution.py:61
  209.4 24.7 %fusion.158 = (f32[8,784]{1,0:T(8,128)S(1)}, f32[8,784]{1,0:T(8,128)S(1)}) fusion(f32[784,256]{1,0:T(8,128)S(1)} %multiply_add_fusion.13, f32[8]{0:T(128)S(1)} %fusion.157, f32[256]{0:T(256)S(1)} %bitcast.407), kind=kLoop, calls=%fused_computation.132.clone.1 | loop fusion | flops 8015616 | bytes 854048 | tf_op jit(solution)/shard_map/while/body/eval_jaxpr/reduce_sum | solution.py:61
  234.6 24.7 %fusion.158 = (f32[8,784]{1,0:T(8,128)S(1)}, f32[8,784]{1,0:T(8,128)S(1)}) fusion(f32[784,256]{1,0:T(8,128)S(1)} %multiply_add_fusion.13, f32[8]{0:T(128)S(1)} %fusion.157, f32[256]{0:T(256)S(1)} %bitcast.407), kind=kLoop, calls=%fused_computation.132.clone.1 | loop fusion | flops 8015616 | bytes 854048 | tf_op jit(solution)/shard_map/while/body/eval_jaxpr/reduce_sum | solution.py:61
  262.0 4.1 collective-permute-start.5
  266.2 150.7 %while.88 = (s32[]{:T(128)}, f32[6,2,8,784]{3,2,0,1:T(8,128)S(1)}, f32[1,256]{1,0:T(1,128)S(1)}, f32[6,8]{1,0:T(8,128)S(1)}, f32[256]{0:T(256)S(1)}, /*index=5*/...) while((s32[]{:T(128)}, f32[6,2,8,784]{3,2,0,1:T(8,128)S(1)}, ...), condition=%wide.region_18.21_spmd.clone, body=%wide.region_15.20_spmd.clone.sunk | while | flops 9031682 | bytes 1784213 | solution.py:66
  266.6 24.7 %fusion.155 = (f32[8,784]{1,0:T(8,128)S(1)}, f32[8,784]{1,0:T(8,128)S(1)}) fusion(f32[784,256]{1,0:T(8,128)S(1)} %multiply_add_fusion.12, f32[8]{0:T(128)S(1)} %fusion.154, f32[256]{0:T(256)S(1)} %bitcast.408), kind=kLoop, calls=%fused_computation.121.clone.1 | loop fusion | flops 8015616 | bytes 854048 | tf_op jit(solution)/shard_map/while/body/eval_jaxpr/reduce_sum | solution.py:61
  291.7 24.7 %fusion.155 = (f32[8,784]{1,0:T(8,128)S(1)}, f32[8,784]{1,0:T(8,128)S(1)}) fusion(f32[784,256]{1,0:T(8,128)S(1)} %multiply_add_fusion.12, f32[8]{0:T(128)S(1)} %fusion.154, f32[256]{0:T(256)S(1)} %bitcast.408), kind=kLoop, calls=%fused_computation.121.clone.1 | loop fusion | flops 8015616 | bytes 854048 | tf_op jit(solution)/shard_map/while/body/eval_jaxpr/reduce_sum | solution.py:61
  316.8 24.7 %fusion.155 = (f32[8,784]{1,0:T(8,128)S(1)}, f32[8,784]{1,0:T(8,128)S(1)}) fusion(f32[784,256]{1,0:T(8,128)S(1)} %multiply_add_fusion.12, f32[8]{0:T(128)S(1)} %fusion.154, f32[256]{0:T(256)S(1)} %bitcast.408), kind=kLoop, calls=%fused_computation.121.clone.1 | loop fusion | flops 8015616 | bytes 854048 | tf_op jit(solution)/shard_map/while/body/eval_jaxpr/reduce_sum | solution.py:61
  341.9 24.7 %fusion.155 = (f32[8,784]{1,0:T(8,128)S(1)}, f32[8,784]{1,0:T(8,128)S(1)}) fusion(f32[784,256]{1,0:T(8,128)S(1)} %multiply_add_fusion.12, f32[8]{0:T(128)S(1)} %fusion.154, f32[256]{0:T(256)S(1)} %bitcast.408), kind=kLoop, calls=%fused_computation.121.clone.1 | loop fusion | flops 8015616 | bytes 854048 | tf_op jit(solution)/shard_map/while/body/eval_jaxpr/reduce_sum | solution.py:61
  367.0 24.7 %fusion.155 = (f32[8,784]{1,0:T(8,128)S(1)}, f32[8,784]{1,0:T(8,128)S(1)}) fusion(f32[784,256]{1,0:T(8,128)S(1)} %multiply_add_fusion.12, f32[8]{0:T(128)S(1)} %fusion.154, f32[256]{0:T(256)S(1)} %bitcast.408), kind=kLoop, calls=%fused_computation.121.clone.1 | loop fusion | flops 8015616 | bytes 854048 | tf_op jit(solution)/shard_map/while/body/eval_jaxpr/reduce_sum | solution.py:61
  392.1 24.7 %fusion.155 = (f32[8,784]{1,0:T(8,128)S(1)}, f32[8,784]{1,0:T(8,128)S(1)}) fusion(f32[784,256]{1,0:T(8,128)S(1)} %multiply_add_fusion.12, f32[8]{0:T(128)S(1)} %fusion.154, f32[256]{0:T(256)S(1)} %bitcast.408), kind=kLoop, calls=%fused_computation.121.clone.1 | loop fusion | flops 8015616 | bytes 854048 | tf_op jit(solution)/shard_map/while/body/eval_jaxpr/reduce_sum | solution.py:61
  419.2 16.2 %while.86 = (s32[]{:T(128)}, f32[8,3,8,128]{3,2,1,0:T(8,128)S(1)}, f32[8,4,8,128]{3,2,1,0:T(8,128)S(1)}, f32[8,4,8,512]{3,2,0,1:T(8,128)S(1)}, s32[]{:T(128)}, /*index=5*/s32[]{:T(128)}, s32[]{}, s32[]{}, s32[]{}) while((s32[]{:T(128)}, f32[8,3,8,128]{3,2,1,0:T(8,128)S(1)}, f32[8,4,8,128]{3,2,1,0:T(8,128)S(1)}, ...), condition=%wide.region_14.16_spmd, body=%wide.region_10.15_spmd.sunk | while | flops 8916997 | bytes 413849 | solution.py:137
  435.5 2.7 copy.185
  438.2 8.7 %fusion.73 = f32[3,8192]{0,1:T(8,128)} fusion(f32[3,8,8,128]{0,3,2,1:T(8,128)} %copy.185, f32[8192]{0:T(1024)S(1)} %bitcast.373, f32[3,8,8,128]{0,3,2,1:T(8,128)} %copy.178, f32[3,8,8,128]{0,3,2,1:T(8,128)} %copy.171, f32[1,3,8192]{1,2,0:T(8,128)} %copy.164), kind=kLoop, calls=%fused_computation.169 | loop fusion | flops 147456 | bytes 524288 | tf_op jit(solution)/shard_map/add.2
  449.0 11.4 %all-gather.3.cloned.1.call-done = f32[8,2,48,784]{3,2,1,0:T(8,128)} async-done(((f32[1,2,48,784]{3,2,1,0:T(8,128)}), f32[8,2,48,784]{3,2,1,0:T(8,128)}) %all-gather.3.cloned.1.call-update) | async-done | bytes 2408464 | tf_op jit(solution)/shard_map/all_gather | solution.py:170
  462.6 34.5 %all-reduce = (f32[48]{0:T(128)S(1)}, f32[48]{0:T(128)S(1)}) all-reduce(f32[48]{0:T(128)S(1)} %broadcast_multiply_fusion.5, f32[48]{0:T(128)S(1)} %broadcast_multiply_fusion.4), channel_id=1, replica_groups=mesh['rep'=16,'sp'=8] {'rep'}, use_global_device_ids=true, to_apply=%region_21.24 | all-reduce | flops 96 | bytes 768 | tf_op jit(solution)/shard_map/psum | solution.py:172
  497.2 146.9 %while.91 = (s32[]{:T(128)}, f32[784,256]{1,0:T(8,128)S(1)}, f32[6,8]{1,0:T(8,128)S(1)}, f32[6,8,784]{2,1,0:T(8,128)S(1)}, f32[6,8,784]{2,1,0:T(8,128)S(1)}, /*i...) while((s32[]{:T(128)}, f32[784,256]{1,0:T(8,128)S(1)}, ...), condition=%wide.region_43.46_spmd.clone, body=%wide.region_41.45_spmd.clone.sunk | while | flops 10838019 | bytes 4980143 | solution.py:94
  497.6 23.8 %fusion.163 = f32[784,256]{1,0:T(8,128)S(1)} fusion(f32[8,784]{1,0:T(8,128)S(1)} %get-tuple-element.1132, f32[784,256]{1,0:T(8,128)S(1)} %multiply_add_fusion.15, f32[8,784]{1,0:T(8,128)S(1)} %get-tuple-element.1133, f32[8]{0:T(128)S(1)} %fusion.162), kind=kLoop, calls=%fused_computation.158.clone.1 | loop fusion | flops 9433088 | bytes 1655840 | tf_op jit(solution)/shard_map/while/body/eval_jaxpr/reduce_sum | solution.py:87
  522.1 23.8 %fusion.163 = f32[784,256]{1,0:T(8,128)S(1)} fusion(f32[8,784]{1,0:T(8,128)S(1)} %get-tuple-element.1132, f32[784,256]{1,0:T(8,128)S(1)} %multiply_add_fusion.15, f32[8,784]{1,0:T(8,128)S(1)} %get-tuple-element.1133, f32[8]{0:T(128)S(1)} %fusion.162), kind=kLoop, calls=%fused_computation.158.clone.1 | loop fusion | flops 9433088 | bytes 1655840 | tf_op jit(solution)/shard_map/while/body/eval_jaxpr/reduce_sum | solution.py:87
  546.6 23.8 %fusion.163 = f32[784,256]{1,0:T(8,128)S(1)} fusion(f32[8,784]{1,0:T(8,128)S(1)} %get-tuple-element.1132, f32[784,256]{1,0:T(8,128)S(1)} %multiply_add_fusion.15, f32[8,784]{1,0:T(8,128)S(1)} %get-tuple-element.1133, f32[8]{0:T(128)S(1)} %fusion.162), kind=kLoop, calls=%fused_computation.158.clone.1 | loop fusion | flops 9433088 | bytes 1655840 | tf_op jit(solution)/shard_map/while/body/eval_jaxpr/reduce_sum | solution.py:87
  571.1 23.8 %fusion.163 = f32[784,256]{1,0:T(8,128)S(1)} fusion(f32[8,784]{1,0:T(8,128)S(1)} %get-tuple-element.1132, f32[784,256]{1,0:T(8,128)S(1)} %multiply_add_fusion.15, f32[8,784]{1,0:T(8,128)S(1)} %get-tuple-element.1133, f32[8]{0:T(128)S(1)} %fusion.162), kind=kLoop, calls=%fused_computation.158.clone.1 | loop fusion | flops 9433088 | bytes 1655840 | tf_op jit(solution)/shard_map/while/body/eval_jaxpr/reduce_sum | solution.py:87
  595.5 23.8 %fusion.163 = f32[784,256]{1,0:T(8,128)S(1)} fusion(f32[8,784]{1,0:T(8,128)S(1)} %get-tuple-element.1132, f32[784,256]{1,0:T(8,128)S(1)} %multiply_add_fusion.15, f32[8,784]{1,0:T(8,128)S(1)} %get-tuple-element.1133, f32[8]{0:T(128)S(1)} %fusion.162), kind=kLoop, calls=%fused_computation.158.clone.1 | loop fusion | flops 9433088 | bytes 1655840 | tf_op jit(solution)/shard_map/while/body/eval_jaxpr/reduce_sum | solution.py:87
  620.0 23.8 %fusion.163 = f32[784,256]{1,0:T(8,128)S(1)} fusion(f32[8,784]{1,0:T(8,128)S(1)} %get-tuple-element.1132, f32[784,256]{1,0:T(8,128)S(1)} %multiply_add_fusion.15, f32[8,784]{1,0:T(8,128)S(1)} %get-tuple-element.1133, f32[8]{0:T(128)S(1)} %fusion.162), kind=kLoop, calls=%fused_computation.158.clone.1 | loop fusion | flops 9433088 | bytes 1655840 | tf_op jit(solution)/shard_map/while/body/eval_jaxpr/reduce_sum | solution.py:87
  644.2 146.9 %while.90 = (s32[]{:T(128)}, f32[784,256]{1,0:T(8,128)S(1)}, f32[6,8]{1,0:T(8,128)S(1)}, f32[6,8,784]{2,1,0:T(8,128)S(1)}, f32[6,8,784]{2,1,0:T(8,128)S(1)}, /*i...) while((s32[]{:T(128)}, f32[784,256]{1,0:T(8,128)S(1)}, ...), condition=%wide.region_24.27_spmd.clone, body=%wide.region_22.26_spmd.clone.sunk | while | flops 10838019 | bytes 4980143 | solution.py:94
  644.6 23.8 %fusion.161 = f32[784,256]{1,0:T(8,128)S(1)} fusion(f32[8,784]{1,0:T(8,128)S(1)} %get-tuple-element.1119, f32[784,256]{1,0:T(8,128)S(1)} %multiply_add_fusion.14, f32[8,784]{1,0:T(8,128)S(1)} %get-tuple-element.1120, f32[8]{0:T(128)S(1)} %fusion.160), kind=kLoop, calls=%fused_computation.145.clone.1 | loop fusion | flops 9433088 | bytes 1655840 | tf_op jit(solution)/shard_map/while/body/eval_jaxpr/reduce_sum | solution.py:87
  669.1 23.8 %fusion.161 = f32[784,256]{1,0:T(8,128)S(1)} fusion(f32[8,784]{1,0:T(8,128)S(1)} %get-tuple-element.1119, f32[784,256]{1,0:T(8,128)S(1)} %multiply_add_fusion.14, f32[8,784]{1,0:T(8,128)S(1)} %get-tuple-element.1120, f32[8]{0:T(128)S(1)} %fusion.160), kind=kLoop, calls=%fused_computation.145.clone.1 | loop fusion | flops 9433088 | bytes 1655840 | tf_op jit(solution)/shard_map/while/body/eval_jaxpr/reduce_sum | solution.py:87
  693.6 23.8 %fusion.161 = f32[784,256]{1,0:T(8,128)S(1)} fusion(f32[8,784]{1,0:T(8,128)S(1)} %get-tuple-element.1119, f32[784,256]{1,0:T(8,128)S(1)} %multiply_add_fusion.14, f32[8,784]{1,0:T(8,128)S(1)} %get-tuple-element.1120, f32[8]{0:T(128)S(1)} %fusion.160), kind=kLoop, calls=%fused_computation.145.clone.1 | loop fusion | flops 9433088 | bytes 1655840 | tf_op jit(solution)/shard_map/while/body/eval_jaxpr/reduce_sum | solution.py:87
  718.1 23.8 %fusion.161 = f32[784,256]{1,0:T(8,128)S(1)} fusion(f32[8,784]{1,0:T(8,128)S(1)} %get-tuple-element.1119, f32[784,256]{1,0:T(8,128)S(1)} %multiply_add_fusion.14, f32[8,784]{1,0:T(8,128)S(1)} %get-tuple-element.1120, f32[8]{0:T(128)S(1)} %fusion.160), kind=kLoop, calls=%fused_computation.145.clone.1 | loop fusion | flops 9433088 | bytes 1655840 | tf_op jit(solution)/shard_map/while/body/eval_jaxpr/reduce_sum | solution.py:87
  742.5 23.8 %fusion.161 = f32[784,256]{1,0:T(8,128)S(1)} fusion(f32[8,784]{1,0:T(8,128)S(1)} %get-tuple-element.1119, f32[784,256]{1,0:T(8,128)S(1)} %multiply_add_fusion.14, f32[8,784]{1,0:T(8,128)S(1)} %get-tuple-element.1120, f32[8]{0:T(128)S(1)} %fusion.160), kind=kLoop, calls=%fused_computation.145.clone.1 | loop fusion | flops 9433088 | bytes 1655840 | tf_op jit(solution)/shard_map/while/body/eval_jaxpr/reduce_sum | solution.py:87
  767.0 23.8 %fusion.161 = f32[784,256]{1,0:T(8,128)S(1)} fusion(f32[8,784]{1,0:T(8,128)S(1)} %get-tuple-element.1119, f32[784,256]{1,0:T(8,128)S(1)} %multiply_add_fusion.14, f32[8,784]{1,0:T(8,128)S(1)} %get-tuple-element.1120, f32[8]{0:T(128)S(1)} %fusion.160), kind=kLoop, calls=%fused_computation.145.clone.1 | loop fusion | flops 9433088 | bytes 1655840 | tf_op jit(solution)/shard_map/while/body/eval_jaxpr/reduce_sum | solution.py:87
  791.6 5.9 scatter_fusion
  797.6 5.9 multiply_add_fusion.4
  803.4 2.8 copy.188
  806.4 4.0 collective-permute-start.6
  810.4 2.2 collective-permute-start.7
  812.7 5.9 collective-permute-done.7
  820.2 16.2 %while.87 = (s32[]{:T(128)}, f32[8,3,8,128]{3,2,1,0:T(8,128)S(1)}, f32[8,4,8,128]{3,2,1,0:T(8,128)S(1)}, f32[8,4,8,512]{3,2,0,1:T(8,128)S(1)}, s32[]{:T(128)}, /*index=5*/s32[]{:T(128)}, s32[]{}, s32[]{}, s32[]{}) while((s32[]{:T(128)}, f32[8,3,8,128]{3,2,1,0:T(8,128)S(1)}, f32[8,4,8,128]{3,2,1,0:T(8,128)S(1)}, ...), condition=%wide.region_33.36_spmd, body=%wide.region_29.35_spmd.sunk | while | flops 8916997 | bytes 413849 | solution.py:137
  836.5 2.7 copy.193
  839.2 7.7 add_bitcast_fusion
  846.8 5.9 scatter_fusion.1
  852.7 3.5 copy.197
  856.2 3.5 copy.196
  (375 shorter events, 94.1 us)
Async XLA Ops:
  7.2 6.4 copy-start.1
  7.2 12.3 %copy-start.5 = (s32[1,4,64,4]{2,3,1,0:T(4,128)S(1)}, s32[1,4,64,4]{2,3,1,0:T(4,128)}, u32[]{:S(2)}) copy-start(s32[1,4,64,4]{2,3,1,0:T(4,128)} %param.33) | copy-start | bytes 12292
  7.2 12.8 %copy-start.6 = (s32[1,256]{1,0:T(1,128)S(1)}, s32[1,256]{1,0:T(1,128)}, u32[]{:S(2)}) copy-start(s32[1,256]{1,0:T(1,128)} %param.34) | copy-start | bytes 3076
  7.2 13.4 %copy-start = (f32[1,8192]{1,0:T(1,128)S(1)}, f32[1,8192]{1,0:T(1,128)}, u32[]{:S(2)}) copy-start(f32[1,8192]{1,0:T(1,128)} %param.32) | copy-start | bytes 98308
  7.2 13.5 %copy-start.4 = (f32[1,3,8192]{2,0,1:T(1,128)S(1)}, f32[1,3,8192]{2,0,1:T(1,128)}, u32[]{:S(2)}) copy-start(f32[1,3,8192]{2,0,1:T(1,128)} %param.30) | copy-start | bytes 294916
  7.2 439.7 %all-gather.5.cloned.1.call-start = ((), (), s32[]{:S(2)}) async-start(), calls=%async_computation.1 | async-start | bytes 3096576 | tf_op jit(solution)/shard_map/all_gather | solution.py:170
  10.7 17.9 %copy-start.2 = (f32[1,3,8192]{2,0,1:T(1,128)S(1)}, f32[1,3,8192]{2,0,1:T(1,128)}, u32[]{:S(2)}) copy-start(f32[1,3,8192]{2,0,1:T(1,128)} %param.29) | copy-start | bytes 294916
  13.6 15.0 %collective-permute-start = (f32[4,4096]{1,0:T(4,128)S(1)}, f32[4,4096]{1,0:T(4,128)S(1)}, u32[]{:S(2)}, u32[]{:S(2)}) collective-permute-start(f32[4,4096]{1,0:T(4,128)S(1)} %get-tuple-element.651), channel_id=1, source_target_pairs={{0,1},{1,2},{2,3},{3,4},{4,5},{5,6},{6,7},{8,9},{9,10},{10,11},{11... | collective-permute-start | bytes 196616 | tf_op jit(solution)/shard_map/ppermute | solution.py:25
  17.1 11.5 %collective-permute-start.1 = (f32[4,4096]{1,0:T(4,128)S(1)}, f32[4,4096]{1,0:T(4,128)S(1)}, u32[]{:S(2)}, u32[]{:S(2)}) collective-permute-start(f32[4,4096]{1,0:T(4,128)S(1)} %get-tuple-element.652), channel_id=1, source_target_pairs={{1,0},{2,1},{3,2},{4,3},{5,4},{6,5},{7,6},{9,8},{10,9},{11,10},{12... | collective-permute-start | bytes 196616 | tf_op jit(solution)/shard_map/ppermute | solution.py:27
  59.1 8.1 collective-permute-start.2
  64.7 8.3 collective-permute-start.3
  102.0 5.9 copy-start.3
  102.0 6.6 copy-start.7
  260.0 200.4 %all-gather.3.cloned.1.call-start = ((), (), s32[]{:S(2)}) async-start(), calls=%async_computation | async-start | bytes 3096576 | tf_op jit(solution)/shard_map/all_gather | solution.py:170
  260.1 157.5 %collective-permute-start.4 = (f32[4,4096]{1,0:T(4,128)S(1)}, f32[4,4096]{1,0:T(4,128)S(1)}, u32[]{:S(2)}, u32[]{:S(2)}) collective-permute-start(f32[4,4096]{1,0:T(4,128)S(1)} %get-tuple-element.647), channel_id=1, source_target_pairs={{0,1},{1,2},{2,3},{3,4},{4,5},{5,6},{6,7},{8,9},{9,10},{10,11},{11... | collective-permute-start | bytes 196616 | tf_op jit(solution)/shard_map/ppermute | solution.py:25
  262.0 155.6 %collective-permute-start.5 = (f32[4,4096]{1,0:T(4,128)S(1)}, f32[4,4096]{1,0:T(4,128)S(1)}, u32[]{:S(2)}, u32[]{:S(2)}) collective-permute-start(f32[4,4096]{1,0:T(4,128)S(1)} %get-tuple-element.648), channel_id=1, source_target_pairs={{1,0},{2,1},{3,2},{4,3},{5,4},{6,5},{7,6},{9,8},{10,9},{11,10},{12... | collective-permute-start | bytes 196616 | tf_op jit(solution)/shard_map/ppermute | solution.py:27
  446.9 50.2 %copy-start.8 = (f32[48]{0:T(128)S(1)}, f32[48]{0:T(128)}, u32[]{:S(2)}) copy-start(f32[48]{0:T(128)} %param.36) | copy-start | bytes 580
  446.9 50.2 %copy-start.9 = (f32[48]{0:T(128)S(1)}, f32[48]{0:T(128)}, u32[]{:S(2)}) copy-start(f32[48]{0:T(128)} %param.37) | copy-start | bytes 580
  806.4 6.3 collective-permute-start.6
  810.4 8.3 collective-permute-start.7
Sparse Core Ops, SparseCore 0:
  260.2 42.6 all-gather.4
  417.7 42.6 all-gather.2
